TPU v7x, 32 devices: a whole 2x2x4 slice. The times are simulated.
32 devices in a mesh: dp: 4 (over z), row: 2 (over x), col: 4 (over y, core).
Axes of the slice: x: 2, y: 2, z: 4, core: 2. Of those that a mesh axis runs over, the one named last changes fastest.
Arguments:
- inputs: bfloat16 [4096, 1024], P(('dp', 'col'), 'row'), may hold values from -12 to 12
- qkv_weight: bfloat16 [1024, 3, 1024], P('row', None, 'col'), may hold values from -10 to 10
- qv_bias: float32 [2, 1024], P(None, 'col'), may hold values from -3 to 3
- out_weight: bfloat16 [1024, 1024], P('col', 'row'), may hold values from -1 to 1
- out_bias: float32 [1024], P('row'), may hold values from -3 to 3
- first_gain: float32 [1024], P('row'), may hold values from 0.1 to 1.9
- first_shift: float32 [1024], P('row'), may hold values from -3 to 3
- up_weight: bfloat16 [1024, 4096], P('row', 'col'), may hold values from -0.1875 to 0.1875
- up_bias: float32 [4096], P('col'), may hold values from -3 to 3
- down_weight: bfloat16 [4096, 1024], P('col', 'row'), may hold values from -0.09375 to 0.09375
- down_bias: float32 [1024], P('row'), may hold values from -3 to 3
- second_gain: float32 [1024], P('row'), may hold values from 0.1 to 1.9
- second_shift: float32 [1024], P('row'), may hold values from -3 to 3
- lengths: int32 [8], P(('dp', 'row')), may hold values from 128 to 512, as said below
- out_grad: bfloat16 [4096, 1024], P(('dp', 'col'), 'row'), may hold values from -9 to 9
Outputs:
- block_out: bfloat16 [4096, 1024], P(('dp', 'col'), 'row')
- grad_inputs: float32 [4096, 1024], P(('dp', 'col'), 'row')
- grad_qkv_weight: float32 [1024, 3, 1024], P('row', None, 'col')
- grad_qv_bias: float32 [2, 1024], P(None, 'col')
- grad_out_weight: float32 [1024, 1024], P('col', 'row')
- grad_out_bias: float32 [1024], P('row')
- grad_first_gain: float32 [1024], P('row')
- grad_first_shift: float32 [1024], P('row')
- grad_up_weight: float32 [1024, 4096], P('row', 'col')
- grad_up_bias: float32 [4096], P('col')
- grad_down_weight: float32 [4096, 1024], P('col', 'row')
- grad_down_bias: float32 [1024], P('row')
- grad_second_gain: float32 [1024], P('row')
- grad_second_shift: float32 [1024], P('row')
Inputs may be any that keep to these rules, and one draw needn't show every extreme that they name: `lengths`: positions at or past a sequence's length are padding.
All inputs are finite; a program needn't handle non-finite values.
Results may differ from a plain program's by a relative error of at most 0.013.
The roundings to bfloat16 on the way count: a program that leaves them out, or rounds other values in their place, can miss the bound.
Values may be sent and summed in bfloat16 or wider, within the bound.
A program may use at most 128 MiB of HBM per device.

v0:
```python
import jax
import jax.numpy as jnp
from jax import lax
from jax.sharding import PartitionSpec as P

MODEL_WIDTH = 1024
HEADS = 16
HEAD_DIM = 64
L = 512
norm_epsilon = 1e-12
masked_score = -1e30
root_half = 0.7071067811865476
gauss_height = 0.3989422804014327


def forward_gather(block):
    return lax.all_gather(block, "col", axis=0, tiled=True)


def forward_reduce(product_term, row_count):
    return lax.psum_scatter(
        product_term(jnp.int32(0), row_count * lax.axis_size("row")),
        "row",
        scatter_dimension=0,
        tiled=True,
    )


def forward_collect(block):
    return lax.all_gather(block, "row", axis=0, tiled=True)


def forward_combine(product_term, row_count):
    return lax.psum_scatter(
        product_term(jnp.int32(0), row_count * lax.axis_size("col")),
        "col",
        scatter_dimension=0,
        tiled=True,
    )


def backward_gather(block):
    return lax.all_gather(block, "col", axis=0, tiled=True)


def backward_reduce(product_term, row_count):
    return lax.psum_scatter(
        product_term(jnp.int32(0), row_count * lax.axis_size("row")),
        "row",
        scatter_dimension=0,
        tiled=True,
    )


def backward_collect(block):
    return lax.all_gather(block, "row", axis=0, tiled=True)


def backward_combine(product_term, row_count):
    return lax.psum_scatter(
        product_term(jnp.int32(0), row_count * lax.axis_size("col")),
        "col",
        scatter_dimension=0,
        tiled=True,
    )


def width_pair(first_part, second_part):
    return lax.psum((first_part, second_part), "row")


def rows_times(gathered, weight):

    def product_term(first_row, row_count):
        return jnp.dot(gathered, weight, preferred_element_type=jnp.float32)

    return product_term


def rows_times_turned(gathered, weight):

    def product_term(first_row, row_count):
        return lax.dot_general(
            gathered, weight, (((1,), (1,)), ((), ())), preferred_element_type=jnp.float32
        )

    return product_term


def contract_rows(first_side, second_side):
    return lax.dot_general(
        first_side, second_side, (((0,), (0,)), ((), ())), preferred_element_type=jnp.float32
    )


def gelu_pair(preact):
    lower_mass = 0.5 * (1.0 + lax.erf(preact * root_half))
    return (
        preact * lower_mass,
        lower_mass + preact * jnp.exp(-0.5 * preact * preact) * gauss_height,
    )


def norm_forward(hidden, norm_gain, norm_shift):
    center, square = width_pair(
        jnp.sum(hidden, axis=-1, keepdims=True), jnp.sum(hidden * hidden, axis=-1, keepdims=True)
    )
    center = center / MODEL_WIDTH
    square = square / MODEL_WIDTH
    rscale = lax.rsqrt(square - center * center + norm_epsilon)
    normed = (hidden - center) * rscale
    return (normed * norm_gain + norm_shift, normed, rscale)


def norm_back(incoming_gradient, normed, rscale, norm_gain):
    scaled = incoming_gradient * norm_gain
    first_mean, second_mean = width_pair(
        jnp.sum(scaled, axis=-1, keepdims=True), jnp.sum(scaled * normed, axis=-1, keepdims=True)
    )
    return rscale * (scaled - first_mean / MODEL_WIDTH - normed * (second_mean / MODEL_WIDTH))


def score_block(queries, keys_low, lengths):
    scores = jnp.einsum(
        "sqhd,skhd->shqk", queries, keys_low, preferred_element_type=jnp.float32
    ) * HEAD_DIM ** (-0.5)
    visible = lax.broadcasted_iota(jnp.int32, (1, 1, 1, L), 3) < lengths[:, None, None, None]
    return jnp.where(visible, scores, masked_score)


def attend(queries, keys_low, values, lengths):
    scores = score_block(queries, keys_low, lengths)
    row_peak = jnp.max(scores, axis=3, keepdims=True)
    logsum = row_peak + jnp.log(jnp.sum(jnp.exp(scores - row_peak), axis=3, keepdims=True))
    soft_weights = jnp.exp(scores - logsum).astype(jnp.bfloat16)
    attention_output = jnp.einsum(
        "shqk,skhd->sqhd", soft_weights, values, preferred_element_type=jnp.float32
    )
    return (attention_output.astype(jnp.bfloat16), logsum)


def attend_back(queries, keys_low, values, logsum, incoming_gradient, lengths):
    scores = score_block(queries, keys_low, lengths)
    soft_weights = jnp.exp(scores - logsum)
    grad_weights = jnp.einsum(
        "sqhd,skhd->shqk", incoming_gradient, values, preferred_element_type=jnp.float32
    )
    row_inner = jnp.sum(soft_weights * grad_weights, axis=3, keepdims=True)
    score_grad = (soft_weights * (grad_weights - row_inner)).astype(jnp.bfloat16)
    score_scale = HEAD_DIM ** (-0.5)
    grad_queries = (
        jnp.einsum("shqk,skhd->sqhd", score_grad, keys_low, preferred_element_type=jnp.float32)
        * score_scale
    )
    grad_keys = (
        jnp.einsum("shqk,sqhd->skhd", score_grad, queries, preferred_element_type=jnp.float32)
        * score_scale
    )
    grad_values = jnp.einsum(
        "shqk,sqhd->skhd",
        soft_weights.astype(jnp.bfloat16),
        incoming_gradient,
        preferred_element_type=jnp.float32,
    )
    return (grad_queries, grad_keys, grad_values)


def shards(
    inputs,
    qkv_weight,
    qv_bias,
    out_weight,
    out_bias,
    first_gain,
    first_shift,
    up_weight,
    up_bias,
    down_weight,
    down_bias,
    second_gain,
    second_shift,
    lengths,
    out_grad,
):
    head_local = HEADS // lax.axis_size("col")
    seq_local = lengths.shape[0]
    head_shape = (seq_local, L, head_local, HEAD_DIM)
    qkv_flat = qkv_weight.reshape(qkv_weight.shape[0], -1)
    across_rows = inputs.shape[0]
    gathered_in = forward_gather(inputs)
    down_rows = gathered_in.shape[0] // lax.axis_size("row")
    projected = forward_reduce(rows_times(gathered_in, qkv_flat), down_rows).reshape(
        down_rows, 3, -1
    )
    queries = (projected[:, 0] + qv_bias[0]).astype(jnp.bfloat16).reshape(head_shape)
    keys_low = projected[:, 1].astype(jnp.bfloat16).reshape(head_shape)
    values = (projected[:, 2] + qv_bias[1]).astype(jnp.bfloat16).reshape(head_shape)
    attention_output, logsum = attend(queries, keys_low, values, lengths)
    gathered_att = forward_collect(attention_output.reshape(down_rows, -1))
    first_sum = (
        inputs.astype(jnp.float32)
        + forward_combine(rows_times(gathered_att, out_weight), across_rows)
        + out_bias
    )
    first_norm, first_standardized, first_scale = norm_forward(first_sum, first_gain, first_shift)
    gathered_norm = forward_gather(first_norm.astype(jnp.bfloat16))
    preact = forward_reduce(rows_times(gathered_norm, up_weight), down_rows) + up_bias
    activated, gelu_slope = gelu_pair(preact)
    gathered_act = forward_collect(activated.astype(jnp.bfloat16))
    second_sum = (
        first_norm + forward_combine(rows_times(gathered_act, down_weight), across_rows) + down_bias
    )
    second_norm, second_standardized, second_scale = norm_forward(
        second_sum, second_gain, second_shift
    )
    block_out = second_norm.astype(jnp.bfloat16)
    incoming_gradient = out_grad.astype(jnp.float32)
    second_norm_gradient = norm_back(
        incoming_gradient, second_standardized, second_scale, second_gain
    )
    gathered_grad = backward_gather(second_norm_gradient.astype(jnp.bfloat16))
    grad_down = contract_rows(gathered_act, gathered_grad)
    preactivation_gradient = (
        backward_reduce(rows_times_turned(gathered_grad, down_weight), down_rows) * gelu_slope
    )
    gathered_pre = backward_collect(preactivation_gradient.astype(jnp.bfloat16))
    grad_up = contract_rows(gathered_norm, gathered_pre)
    norm_gradient_total = second_norm_gradient + backward_combine(
        rows_times_turned(gathered_pre, up_weight), across_rows
    )
    first_norm_gradient = norm_back(
        norm_gradient_total, first_standardized, first_scale, first_gain
    )
    gathered_first = backward_gather(first_norm_gradient.astype(jnp.bfloat16))
    grad_out = contract_rows(gathered_att, gathered_first)
    attended_grad = (
        backward_reduce(rows_times_turned(gathered_first, out_weight), down_rows)
        .astype(jnp.bfloat16)
        .reshape(head_shape)
    )
    grad_queries, grad_keys, grad_values = attend_back(
        queries, keys_low, values, logsum, attended_grad, lengths
    )
    query_rows_flattened = grad_queries.reshape(down_rows, -1)
    value_rows_flattened = grad_values.reshape(down_rows, -1)
    combined_heads = (
        jnp.stack(
            [query_rows_flattened, grad_keys.reshape(down_rows, -1), value_rows_flattened], axis=1
        )
        .astype(jnp.bfloat16)
        .reshape(down_rows, -1)
    )
    gathered_joined = backward_collect(combined_heads)
    grad_qkv = contract_rows(gathered_in, gathered_joined).reshape(qkv_weight.shape)
    grad_inputs = first_norm_gradient + backward_combine(
        rows_times_turned(gathered_joined, qkv_flat), across_rows
    )
    column_sums = lax.psum(
        (
            jnp.sum(first_norm_gradient, axis=0),
            jnp.sum(norm_gradient_total * first_standardized, axis=0),
            jnp.sum(norm_gradient_total, axis=0),
            jnp.sum(second_norm_gradient, axis=0),
            jnp.sum(incoming_gradient * second_standardized, axis=0),
            jnp.sum(incoming_gradient, axis=0),
        ),
        ("dp", "col"),
    )
    row_sums = lax.psum(
        (
            jnp.stack(
                [jnp.sum(query_rows_flattened, axis=0), jnp.sum(value_rows_flattened, axis=0)]
            ),
            jnp.sum(preactivation_gradient, axis=0),
        ),
        ("dp", "row"),
    )
    grad_qkv, grad_out, grad_up, grad_down = (
        lax.psum(grad_qkv.astype(jnp.bfloat16), "dp").astype(jnp.float32),
        lax.psum(grad_out.astype(jnp.bfloat16), "dp").astype(jnp.float32),
        lax.psum(grad_up.astype(jnp.bfloat16), "dp").astype(jnp.float32),
        lax.psum(grad_down.astype(jnp.bfloat16), "dp").astype(jnp.float32),
    )
    return (
        block_out,
        grad_inputs,
        grad_qkv,
        row_sums[0],
        grad_out,
        column_sums[0],
        column_sums[1],
        column_sums[2],
        grad_up,
        row_sums[1],
        grad_down,
        column_sums[3],
        column_sums[4],
        column_sums[5],
    )


def solution(mesh):
    in_specs = (
        P(("dp", "col"), "row"),
        P("row", None, "col"),
        P(None, "col"),
        P("col", "row"),
        P("row"),
        P("row"),
        P("row"),
        P("row", "col"),
        P("col"),
        P("col", "row"),
        P("row"),
        P("row"),
        P("row"),
        P(("dp", "row")),
        P(("dp", "col"), "row"),
    )
    out_specs = (
        P(("dp", "col"), "row"),
        P(("dp", "col"), "row"),
        P("row", None, "col"),
        P(None, "col"),
        P("col", "row"),
        P("row"),
        P("row"),
        P("row"),
        P("row", "col"),
        P("col"),
        P("col", "row"),
        P("row"),
        P("row"),
        P("row"),
    )
    return jax.shard_map(shards, mesh=mesh, in_specs=in_specs, out_specs=out_specs, check_vma=False)
```

profile of v0, /device:TPU:0, one launch (start us, length us, event | category | flops | bytes accessed | tf_op | source)
XLA Modules:
  0.0 701.3 jit_solution(1587023572651374637)
XLA Ops:
  9.4 19.6 %all-gather.8.cloned.1.call-done = bf16[1024,512]{1,0:T(8,128)(2,1)} async-done(((bf16[256,512]{1,0:T(8,128)(2,1)}), bf16[1024,512]{1,0:T(8,128)(2,1)}) %all-gather.8.cloned.1.call-update) | async-done | bytes 1048592 | tf_op jit(solution)/shard_map/all_gather | solution.py:17
  33.9 42.7 %reduce-scatter.9.cloned.1.call-done = f32[512,768]{1,0:T(8,128)} async-done(((f32[1024,768]{1,0:T(8,128)}), f32[512,768]{1,0:T(8,128)}) %reduce-scatter.9.cloned.1.call-update) | async-done | bytes 1572880 | tf_op jit(solution)/shard_map/reduce_scatter | solution.py:21
  83.1 8.5 %all_gather.25 = bf16[1024,256]{0,1:T(8,128)(2,1)S(1)} all-gather(bf16[512,256]{0,1:T(8,128)(2,1)S(1)} %bitcast.93), channel_id=1, replica_groups=mesh['dp'=4,'row'=2,'col'=4] {'row'}, dimensions={0}, use_global_device_ids=true | all-gather | bytes 786432 | tf_op jit(solution)/shard_map/all_gather | solution.py:30
  94.3 31.3 %reduce-scatter.11.cloned.1.call-done = f32[256,512]{1,0:T(8,128)} async-done(((f32[1024,512]{1,0:T(8,128)}), f32[256,512]{1,0:T(8,128)}) %reduce-scatter.11.cloned.1.call-update) | async-done | bytes 524304 | tf_op jit(solution)/shard_map/reduce_scatter | solution.py:34
  127.6 4.9 all-reduce.5
  134.5 16.8 %all-gather.10.cloned.1.call-done = bf16[1024,512]{1,0:T(8,128)(2,1)} async-done(((bf16[256,512]{1,0:T(8,128)(2,1)}), bf16[1024,512]{1,0:T(8,128)(2,1)}) %all-gather.10.cloned.1.call-update) | async-done | bytes 1048592 | tf_op jit(solution)/shard_map/all_gather | solution.py:17
  151.3 4.8 fusion.31
  156.1 54.5 %reduce-scatter.13.cloned.1.call-done = f32[512,1024]{1,0:T(8,128)} async-done(((f32[1024,1024]{1,0:T(8,128)}), f32[512,1024]{1,0:T(8,128)}) %reduce-scatter.13.cloned.1.call-update) | async-done | bytes 2097168 | tf_op jit(solution)/shard_map/reduce_scatter | solution.py:21
  213.7 33.2 %all-gather.12.cloned.1.call-done = bf16[1024,1024]{1,0:T(8,128)(2,1)} async-done(((bf16[512,1024]{1,0:T(8,128)(2,1)}), bf16[1024,1024]{1,0:T(8,128)(2,1)}) %all-gather.12.cloned.1.call-update) | async-done | bytes 2097168 | tf_op jit(solution)/shard_map/all_gather | solution.py:30
  251.1 31.3 %reduce-scatter.15.cloned.1.call-done = f32[256,512]{1,0:T(8,128)} async-done(((f32[1024,512]{1,0:T(8,128)}), f32[256,512]{1,0:T(8,128)}) %reduce-scatter.15.cloned.1.call-update) | async-done | bytes 524304 | tf_op jit(solution)/shard_map/reduce_scatter | solution.py:34
  284.6 4.9 all-reduce.4
  291.0 4.9 all-reduce.3
  299.6 16.8 %all-gather.14.cloned.1.call-done = bf16[1024,512]{1,0:T(8,128)(2,1)} async-done(((bf16[256,512]{1,0:T(8,128)(2,1)}), bf16[1024,512]{1,0:T(8,128)(2,1)}) %all-gather.14.cloned.1.call-update) | async-done | bytes 1048592 | tf_op jit(solution)/shard_map/all_gather | solution.py:43
  321.0 54.5 %reduce-scatter.17.cloned.1.call-done = f32[512,1024]{1,0:T(8,128)} async-done(((f32[1024,1024]{1,0:T(8,128)}), f32[512,1024]{1,0:T(8,128)}) %reduce-scatter.17.cloned.1.call-update) | async-done | bytes 2097168 | tf_op jit(solution)/shard_map/reduce_scatter | solution.py:47
  379.2 33.0 %all-gather.16.cloned.1.call-done = bf16[1024,1024]{1,0:T(8,128)(2,1)} async-done(((bf16[512,1024]{1,0:T(8,128)(2,1)}), bf16[1024,1024]{1,0:T(8,128)(2,1)}) %all-gather.16.cloned.1.call-update) | async-done | bytes 2097168 | tf_op jit(solution)/shard_map/all_gather | solution.py:56
  416.5 31.3 %reduce-scatter.19.cloned.1.call-done = f32[256,512]{1,0:T(8,128)} async-done(((f32[1024,512]{1,0:T(8,128)}), f32[256,512]{1,0:T(8,128)}) %reduce-scatter.19.cloned.1.call-update) | async-done | bytes 524304 | tf_op jit(solution)/shard_map/reduce_scatter | solution.py:60
  449.8 4.9 all-reduce.2
  456.9 16.8 %all-gather.18.cloned.1.call-done = bf16[1024,512]{1,0:T(8,128)(2,1)} async-done(((bf16[256,512]{1,0:T(8,128)(2,1)}), bf16[1024,512]{1,0:T(8,128)(2,1)}) %all-gather.18.cloned.1.call-update) | async-done | bytes 1048592 | tf_op jit(solution)/shard_map/all_gather | solution.py:43
  476.5 20.5 %reduce-scatter.21.cloned.1.call-done = f32[512,256]{1,0:T(8,128)} async-done(((f32[1024,256]{1,0:T(8,128)}), f32[512,256]{1,0:T(8,128)}) %reduce-scatter.21.cloned.1.call-update) | async-done | bytes 524304 | tf_op jit(solution)/shard_map/reduce_scatter | solution.py:47
  514.9 19.4 %all-gather.20.cloned.1.call-done = bf16[1024,768]{0,1:T(8,128)(2,1)} async-done(((bf16[512,768]{0,1:T(8,128)(2,1)}), bf16[1024,768]{0,1:T(8,128)(2,1)}) %all-gather.20.cloned.1.call-update) | async-done | bytes 1572880 | tf_op jit(solution)/shard_map/all_gather | solution.py:56
  541.1 65.0 %all-reduce = (f32[512]{0:T(512)}, f32[512]{0:T(512)}, f32[512]{0:T(512)}, f32[512]{0:T(512)}, f32[512]{0:T(512)}, /*index=5*/f32[512]{0:T(512)}) all-reduce(f32[512]{0:T(512)S(1)} %get-tuple-element.50, f32[512]{0:T(512)S(1)} %get-tuple-element.14, ...), channel_id=1, replica_groups=mesh['dp'=4,'row'=2,'col'=4] {'dp','col'}, use_global_device_ids=true, to_apply=%region_33.34 | all-reduce | flops 3072 | bytes 24576 | tf_op jit(solution)/shard_map/psum | solution.py:258
  606.2 19.9 %all-reduce.1 = (f32[2,256]{1,0:T(2,128)}, f32[1024]{0:T(1024)}) all-reduce(f32[2,256]{1,0:T(2,128)S(1)} %pad_maximum_fusion.1, f32[1024]{0:T(1024)S(1)} %get-tuple-element.52), channel_id=1, replica_groups=mesh['dp'=4,'row'=2,'col'=4] {'dp','row'}, use_global_device_ids=true, to_apply=%region_30.31 | all-reduce | flops 1536 | bytes 12288 | tf_op jit(solution)/shard_map/psum | solution.py:269
  626.1 34.0 %all-reduce.9.cloned.1.call-done = (bf16[512,3,256]{2,0,1:T(8,128)(2,1)}, bf16[256,512]{1,0:T(8,128)(2,1)}, bf16[512,1024]{1,0:T(8,128)(2,1)}, bf16[1024,512]{1,0:T(8,128)(2,1)}) async-done(((bf16[512,3,256]{2,0,1:T(8,128)(2,1)}, bf16[256,512]{1,0:T(8,128)(2,1)}, bf16[512,1024]{1,0:T(8,128)(2,1)}, bf16[1024,512]{1,0:T(8,128)(2,1)}), (bf16[512,3,256]{2,0,1:T(8,128)(2,1)}, bf16[256,512]{1,0:T(8,128)(2,1)}, ...) | async-done | bytes 3145744 | tf_op jit(solution)/shard_map/psum | solution.py:279
  667.5 25.3 %reduce-scatter.23.cloned.1.call-done = f32[256,512]{1,0:T(8,128)} async-done(((f32[1024,512]{1,0:T(8,128)}), f32[256,512]{1,0:T(8,128)}) %reduce-scatter.23.cloned.1.call-update) | async-done | bytes 524304 | tf_op jit(solution)/shard_map/reduce_scatter | solution.py:60
  (159 shorter events, 87.5 us)
Async XLA Ops:
  7.2 239.7 %copy-start = (bf16[1024,512]{1,0:T(8,128)(2,1)S(1)}, bf16[1024,512]{1,0:T(8,128)(2,1)}, u32[]{:S(2)}) copy-start(bf16[1024,512]{1,0:T(8,128)(2,1)} %param.24) | copy-start | bytes 3145732
  7.2 21.8 %all-gather.8.cloned.1.call-start = ((), (), s32[]{:S(2)}) async-start(), calls=%async_computation.8 | async-start | bytes 1310720 | tf_op jit(solution)/shard_map/all_gather | solution.py:17
  7.9 68.6 %reduce-scatter.9.cloned.1.call-start = ((), (), s32[]{:S(2)}) async-start(), calls=%async_computation.9 | async-start | bytes 4718592 | tf_op jit(solution)/shard_map/reduce_scatter | solution.py:21
  33.0 92.6 %reduce-scatter.11.cloned.1.call-start = ((), (), s32[]{:S(2)}) async-start(), calls=%async_computation.10 | async-start | bytes 2621440 | tf_op jit(solution)/shard_map/reduce_scatter | solution.py:34
  92.4 33.2 %copy-start.28 = (f32[512]{0:T(512)S(1)}, f32[512]{0:T(512)}, u32[]{:S(2)}) copy-start(f32[512]{0:T(512)} %param.19) | copy-start | bytes 6148
  94.2 38.3 %copy-start.24 = (f32[512]{0:T(512)S(1)}, f32[512]{0:T(512)}, u32[]{:S(2)}) copy-start(f32[512]{0:T(512)} %param.20) | copy-start | bytes 6148
  94.2 38.3 %copy-start.26 = (f32[512]{0:T(512)S(1)}, f32[512]{0:T(512)}, u32[]{:S(2)}) copy-start(f32[512]{0:T(512)} %param.21) | copy-start | bytes 6148
  94.3 57.0 %all-gather.10.cloned.1.call-start = ((), (), s32[]{:S(2)}) async-start(), calls=%async_computation.11 | async-start | bytes 1310720 | tf_op jit(solution)/shard_map/all_gather | solution.py:17
  134.4 76.2 %reduce-scatter.13.cloned.1.call-start = ((), (), s32[]{:S(2)}) async-start(), calls=%async_computation.12 | async-start | bytes 6291456 | tf_op jit(solution)/shard_map/reduce_scatter | solution.py:21
  156.1 54.6 %copy-start.25 = (f32[1024]{0:T(1024)S(1)}, f32[1024]{0:T(1024)}, u32[]{:S(2)}) copy-start(f32[1024]{0:T(1024)} %param.23) | copy-start | bytes 12292
  156.1 90.8 %all-gather.12.cloned.1.call-start = ((), (), s32[]{:S(2)}) async-start(), calls=%async_computation.13 | async-start | bytes 3145728 | tf_op jit(solution)/shard_map/all_gather | solution.py:30
  213.7 68.8 %reduce-scatter.15.cloned.1.call-start = ((), (), s32[]{:S(2)}) async-start(), calls=%async_computation.14 | async-start | bytes 2621440 | tf_op jit(solution)/shard_map/reduce_scatter | solution.py:34
  251.1 38.5 %copy-start.27 = (f32[512]{0:T(512)S(1)}, f32[512]{0:T(512)}, u32[]{:S(2)}) copy-start(f32[512]{0:T(512)} %param.26) | copy-start | bytes 6148
  251.1 44.9 %copy-start.30 = (f32[512]{0:T(512)S(1)}, f32[512]{0:T(512)}, u32[]{:S(2)}) copy-start(f32[512]{0:T(512)} %param.27) | copy-start | bytes 6148
  251.1 65.4 %all-gather.14.cloned.1.call-start = ((), (), s32[]{:S(2)}) async-start(), calls=%async_computation.15 | async-start | bytes 1310720 | tf_op jit(solution)/shard_map/all_gather | solution.py:43
  299.6 75.9 %reduce-scatter.17.cloned.1.call-start = ((), (), s32[]{:S(2)}) async-start(), calls=%async_computation.16 | async-start | bytes 6291456 | tf_op jit(solution)/shard_map/reduce_scatter | solution.py:47
  320.9 91.3 %copy-start.34 = (bf16[512,1024]{1,0:T(8,128)(2,1)S(1)}, bf16[512,1024]{1,0:T(8,128)(2,1)}, u32[]{:S(2)}) copy-start(bf16[512,1024]{1,0:T(8,128)(2,1)} %param.22) | copy-start | bytes 3145732
  321.0 91.3 %all-gather.16.cloned.1.call-start = ((), (), s32[]{:S(2)}) async-start(), calls=%async_computation.17 | async-start | bytes 3145728 | tf_op jit(solution)/shard_map/all_gather | solution.py:56
  379.0 68.8 %reduce-scatter.19.cloned.1.call-start = ((), (), s32[]{:S(2)}) async-start(), calls=%async_computation.18 | async-start | bytes 2621440 | tf_op jit(solution)/shard_map/reduce_scatter | solution.py:60
  416.5 57.3 %all-gather.18.cloned.1.call-start = ((), (), s32[]{:S(2)}) async-start(), calls=%async_computation.19 | async-start | bytes 1310720 | tf_op jit(solution)/shard_map/all_gather | solution.py:43
  456.9 40.1 %reduce-scatter.21.cloned.1.call-start = ((), (), s32[]{:S(2)}) async-start(), calls=%async_computation.20 | async-start | bytes 1572864 | tf_op jit(solution)/shard_map/reduce_scatter | solution.py:47
  476.5 57.9 %all-gather.20.cloned.1.call-start = ((), (), s32[]{:S(2)}) async-start(), calls=%async_computation.21 | async-start | bytes 2359296 | tf_op jit(solution)/shard_map/all_gather | solution.py:56
  507.0 153.1 %all-reduce.9.cloned.1.call-start = ((), (), s32[]{:S(2)}) async-start(), calls=%async_computation.23 | async-start | bytes 6291456 | tf_op jit(solution)/shard_map/psum | solution.py:279
  537.9 154.9 %reduce-scatter.23.cloned.1.call-start = ((), (), s32[]{:S(2)}) async-start(), calls=%async_computation.22 | async-start | bytes 2621440 | tf_op jit(solution)/shard_map/reduce_scatter | solution.py:60
  (27 other events, 286.8 us)
Sparse Core Ops, SparseCore 0:
  9.6 19.4 all-gather.7
  33.1 43.4 reduce-scatter.8
  94.4 31.1 reduce-scatter.10
  134.6 16.6 all-gather.9
  156.2 54.3 reduce-scatter.12
  213.8 33.0 all-gather.11
  251.2 31.1 reduce-scatter.14
  299.7 16.7 all-gather.13
  321.1 54.3 reduce-scatter.16
  379.1 33.0 all-gather.15
  416.6 31.1 reduce-scatter.18
  457.0 16.7 all-gather.17
  476.6 20.3 reduce-scatter.20
  507.1 27.1 all-gather.19
  538.1 121.9 all-reduce.8
  662.4 30.3 reduce-scatter.22
where the time goes:
time: 702 us; the launch traced here: 701 us
  waiting for transfers between devices  482 us (69%)
  blocking collectives  113 us (16%)
  matrix products  45.8 us (7%)
  other arithmetic  35.5 us (5%)
  between operations  14.9 us (2%)
  local copies, waits for them, and re-layouts  9.27 us (1%)
    reduce_scatter x2, waiting for transfers between devices, forward_reduce(): lax.psum_scatter(product_term(jnp.int32(0), row_count * lax.axis_size('ro...  97.2 us
    reduce_scatter x2, waiting for transfers between devices, backward_reduce(): lax.psum_scatter(product_term(jnp.int32(0), row_count * lax.axis_size('ro...  74.9 us
    psum x1, blocking collectives, shards(): lax.psum((jnp.sum(first_norm_gradient, axis=0), jnp.sum(norm_gradient_tot...  65 us
    reduce_scatter x2, waiting for transfers between devices, forward_combine(): lax.psum_scatter(product_term(jnp.int32(0), row_count * lax.axis_size('co...  62.6 us
    reduce_scatter x2, waiting for transfers between devices, backward_combine(): lax.psum_scatter(product_term(jnp.int32(0), row_count * lax.axis_size('co...  56.5 us
    all_gather x2, waiting for transfers between devices, backward_collect(): return lax.all_gather(block, 'row', axis=0, tiled=True)  52.5 us
    all_gather x2, waiting for transfers between devices, forward_gather(): return lax.all_gather(block, 'col', axis=0, tiled=True)  36.4 us
    psum x1, waiting for transfers between devices, shards(): lax.psum(grad_qkv.astype(jnp.bfloat16), 'dp').astype(jnp.float32)  34 us
  transfers between devices with their start and end apart: 16, of which 16 were waited for; matrix products, arithmetic and copies ran while one was open for 3% of the time, Pallas kernels for 0%

commit v1 on v0

--- a/solution.py
+++ b/solution.py
@@ -13,8 +13,26 @@
 gauss_height = 0.3989422804014327
 
 
+def gather_around(value, axis, dim):
+    ways, here, lap = (lax.axis_size(axis), lax.axis_index(axis), value.shape[dim])
+    dims = [n * ways if d == dim else n for d, n in enumerate(value.shape)]
+    full = lax.dynamic_update_slice_in_dim(
+        jnp.zeros(dims, value.dtype), value, here * lap, axis=dim
+    )
+    going_up = going_down = value
+    for far in range(1, ways // 2 + 1):
+        going_up = lax.ppermute(going_up, axis, [(d, (d + 1) % ways) for d in range(ways)])
+        full = lax.dynamic_update_slice_in_dim(full, going_up, (here - far) % ways * lap, axis=dim)
+        if 2 * far < ways:
+            going_down = lax.ppermute(going_down, axis, [(d, (d - 1) % ways) for d in range(ways)])
+            full = lax.dynamic_update_slice_in_dim(
+                full, going_down, (here + far) % ways * lap, axis=dim
+            )
+    return full
+
+
 def forward_gather(block):
-    return lax.all_gather(block, "col", axis=0, tiled=True)
+    return gather_around(block, "col", 0)
 
 
 def forward_reduce(product_term, row_count):

time: 702 us -> 693 us (0.987)
  waiting for transfers between devices: 482 us -> 465 us
    all_gather x2 -> x0, waiting for transfers between devices: 36.4 us -> none  [forward_gather(): return lax.all_gather(block, 'col', axis=0, tiled=True)]
    ppermute x0 -> x6, waiting for transfers between devices: none -> 17.1 us  [the longest x4 17.1 us: gather_around(): lax.ppermute(going_up, axis, [(d, (d + 1) % ways) for d in range(ways)])]
  transfers between devices with their start and end apart: 16 -> 20, of which waited for: 16 -> 18; matrix products, arithmetic and copies ran while one was open for 3% -> 3% of each run, Pallas kernels for 0% -> 0%
where the time goes in v1:
time: 693 us; the launch traced here: 692 us
  waiting for transfers between devices  465 us (67%)
  blocking collectives  113 us (16%)
  matrix products  43.5 us (6%)
  other arithmetic  32.5 us (5%)
  between operations  15.1 us (2%)
  local copies, waits for them, and re-layouts  14.8 us (2%)
  starting transfers between devices  7.66 us (1%)
    reduce_scatter x2, waiting for transfers between devices, forward_reduce(): lax.psum_scatter(product_term(jnp.int32(0), row_count * lax.axis_size('ro...  101 us
    reduce_scatter x2, waiting for transfers between devices, backward_reduce(): lax.psum_scatter(product_term(jnp.int32(0), row_count * lax.axis_size('ro...  74.8 us
    psum x1, blocking collectives, shards(): lax.psum((jnp.sum(first_norm_gradient, axis=0), jnp.sum(norm_gradient_tot...  64.9 us
    reduce_scatter x2, waiting for transfers between devices, forward_combine(): lax.psum_scatter(product_term(jnp.int32(0), row_count * lax.axis_size('co...  62.5 us
    reduce_scatter x2, waiting for transfers between devices, backward_combine(): lax.psum_scatter(product_term(jnp.int32(0), row_count * lax.axis_size('co...  56.3 us
    all_gather x2, waiting for transfers between devices, backward_collect(): return lax.all_gather(block, 'row', axis=0, tiled=True)  53 us
    all_gather x2, waiting for transfers between devices, backward_gather(): return lax.all_gather(block, 'col', axis=0, tiled=True)  33.6 us
    psum x1, waiting for transfers between devices, shards(): lax.psum(grad_qkv.astype(jnp.bfloat16), 'dp').astype(jnp.float32)  33.4 us
  transfers between devices with their start and end apart: 20, of which 18 were waited for; matrix products, arithmetic and copies ran while one was open for 3% of the time, Pallas kernels for 0%

profile of v1, /device:TPU:0, one launch (start us, length us, event | category | flops | bytes accessed | tf_op | source)
XLA Modules:
  0.0 691.7 jit_solution(16775958046374825187)
XLA Ops:
  24.7 46.5 %reduce-scatter.9.cloned.1.call-done = f32[512,768]{1,0:T(8,128)} async-done(((f32[1024,768]{1,0:T(8,128)}), f32[512,768]{1,0:T(8,128)}) %reduce-scatter.9.cloned.1.call-update) | async-done | bytes 1572880 | tf_op jit(solution)/shard_map/reduce_scatter | solution.py:39
  77.8 8.6 %all_gather.18 = bf16[1024,256]{0,1:T(8,128)(2,1)S(1)} all-gather(bf16[512,256]{0,1:T(8,128)(2,1)S(1)} %bitcast.92), channel_id=1, replica_groups=mesh['dp'=4,'row'=2,'col'=4] {'row'}, dimensions={0}, use_global_device_ids=true | all-gather | bytes 786432 | tf_op jit(solution)/shard_map/all_gather | solution.py:48
  89.0 31.3 %reduce-scatter.11.cloned.1.call-done = f32[256,512]{1,0:T(8,128)} async-done(((f32[1024,512]{1,0:T(8,128)}), f32[256,512]{1,0:T(8,128)}) %reduce-scatter.11.cloned.1.call-update) | async-done | bytes 524304 | tf_op jit(solution)/shard_map/reduce_scatter | solution.py:52
  122.3 4.9 all-reduce.5
  130.4 6.2 collective-permute-done.3
  136.6 5.7 collective-permute-done.5
  146.7 54.3 %reduce-scatter.13.cloned.1.call-done = f32[512,1024]{1,0:T(8,128)} async-done(((f32[1024,1024]{1,0:T(8,128)}), f32[512,1024]{1,0:T(8,128)}) %reduce-scatter.13.cloned.1.call-update) | async-done | bytes 2097168 | tf_op jit(solution)/shard_map/reduce_scatter | solution.py:39
  204.0 33.2 %all-gather.6.cloned.1.call-done = bf16[1024,1024]{1,0:T(8,128)(2,1)} async-done(((bf16[512,1024]{1,0:T(8,128)(2,1)}), bf16[1024,1024]{1,0:T(8,128)(2,1)}) %all-gather.6.cloned.1.call-update) | async-done | bytes 2097168 | tf_op jit(solution)/shard_map/all_gather | solution.py:48
  241.5 31.3 %reduce-scatter.15.cloned.1.call-done = f32[256,512]{1,0:T(8,128)} async-done(((f32[1024,512]{1,0:T(8,128)}), f32[256,512]{1,0:T(8,128)}) %reduce-scatter.15.cloned.1.call-update) | async-done | bytes 524304 | tf_op jit(solution)/shard_map/reduce_scatter | solution.py:52
  274.9 4.9 all-reduce.4
  281.3 4.9 all-reduce.3
  289.9 16.8 %all-gather.8.cloned.1.call-done = bf16[1024,512]{1,0:T(8,128)(2,1)} async-done(((bf16[256,512]{1,0:T(8,128)(2,1)}), bf16[1024,512]{1,0:T(8,128)(2,1)}) %all-gather.8.cloned.1.call-update) | async-done | bytes 1048592 | tf_op jit(solution)/shard_map/all_gather | solution.py:61
  306.7 4.5 fusion.34
  311.5 54.3 %reduce-scatter.17.cloned.1.call-done = f32[512,1024]{1,0:T(8,128)} async-done(((f32[1024,1024]{1,0:T(8,128)}), f32[512,1024]{1,0:T(8,128)}) %reduce-scatter.17.cloned.1.call-update) | async-done | bytes 2097168 | tf_op jit(solution)/shard_map/reduce_scatter | solution.py:65
  369.3 33.2 %all-gather.10.cloned.1.call-done = bf16[1024,1024]{1,0:T(8,128)(2,1)} async-done(((bf16[512,1024]{1,0:T(8,128)(2,1)}), bf16[1024,1024]{1,0:T(8,128)(2,1)}) %all-gather.10.cloned.1.call-update) | async-done | bytes 2097168 | tf_op jit(solution)/shard_map/all_gather | solution.py:74
  406.8 31.3 %reduce-scatter.19.cloned.1.call-done = f32[256,512]{1,0:T(8,128)} async-done(((f32[1024,512]{1,0:T(8,128)}), f32[256,512]{1,0:T(8,128)}) %reduce-scatter.19.cloned.1.call-update) | async-done | bytes 524304 | tf_op jit(solution)/shard_map/reduce_scatter | solution.py:78
  440.1 4.9 all-reduce.2
  447.2 16.8 %all-gather.12.cloned.1.call-done = bf16[1024,512]{1,0:T(8,128)(2,1)} async-done(((bf16[256,512]{1,0:T(8,128)(2,1)}), bf16[1024,512]{1,0:T(8,128)(2,1)}) %all-gather.12.cloned.1.call-update) | async-done | bytes 1048592 | tf_op jit(solution)/shard_map/all_gather | solution.py:61
  466.8 20.5 %reduce-scatter.21.cloned.1.call-done = f32[512,256]{1,0:T(8,128)} async-done(((f32[1024,256]{1,0:T(8,128)}), f32[512,256]{1,0:T(8,128)}) %reduce-scatter.21.cloned.1.call-update) | async-done | bytes 524304 | tf_op jit(solution)/shard_map/reduce_scatter | solution.py:65
  504.9 19.8 %all-gather.14.cloned.1.call-done = bf16[1024,768]{0,1:T(8,128)(2,1)} async-done(((bf16[512,768]{0,1:T(8,128)(2,1)}), bf16[1024,768]{0,1:T(8,128)(2,1)}) %all-gather.14.cloned.1.call-update) | async-done | bytes 1572880 | tf_op jit(solution)/shard_map/all_gather | solution.py:74
  532.1 64.9 %all-reduce = (f32[512]{0:T(512)}, f32[512]{0:T(512)}, f32[512]{0:T(512)}, f32[512]{0:T(512)}, f32[512]{0:T(512)}, /*index=5*/f32[512]{0:T(512)}) all-reduce(f32[512]{0:T(512)S(1)} %get-tuple-element.64, f32[512]{0:T(512)S(1)} %get-tuple-element.28, ...), channel_id=1, replica_groups=mesh['dp'=4,'row'=2,'col'=4] {'dp','col'}, use_global_device_ids=true, to_apply=%region_33.34 | all-reduce | flops 3072 | bytes 24576 | tf_op jit(solution)/shard_map/psum | solution.py:276
  597.2 20.0 %all-reduce.1 = (f32[2,256]{1,0:T(2,128)}, f32[1024]{0:T(1024)}) all-reduce(f32[2,256]{1,0:T(2,128)S(1)} %pad_maximum_fusion.1, f32[1024]{0:T(1024)S(1)} %get-tuple-element.66), channel_id=1, replica_groups=mesh['dp'=4,'row'=2,'col'=4] {'dp','row'}, use_global_device_ids=true, to_apply=%region_30.31 | all-reduce | flops 1536 | bytes 12288 | tf_op jit(solution)/shard_map/psum | solution.py:287
  617.2 33.4 %all-reduce.9.cloned.1.call-done = (bf16[512,3,256]{0,2,1:T(8,128)(2,1)}, bf16[256,512]{1,0:T(8,128)(2,1)}, bf16[512,1024]{1,0:T(8,128)(2,1)}, bf16[1024,512]{1,0:T(8,128)(2,1)}) async-done(((bf16[512,3,256]{0,2,1:T(8,128)(2,1)}, bf16[256,512]{1,0:T(8,128)(2,1)}, bf16[512,1024]{1,0:T(8,128)(2,1)}, bf16[1024,512]{1,0:T(8,128)(2,1)}), (bf16[512,3,256]{0,2,1:T(8,128)(2,1)}, bf16[256,512]{1,0:T(8,128)(2,1)}, ...) | async-done | bytes 3145744 | tf_op jit(solution)/shard_map/psum | solution.py:297
  658.2 25.0 %reduce-scatter.23.cloned.1.call-done = f32[256,512]{1,0:T(8,128)} async-done(((f32[1024,512]{1,0:T(8,128)}), f32[256,512]{1,0:T(8,128)}) %reduce-scatter.23.cloned.1.call-update) | async-done | bytes 524304 | tf_op jit(solution)/shard_map/reduce_scatter | solution.py:78
  (180 shorter events, 99.4 us)
Async XLA Ops:
  7.2 230.1 %copy-start = (bf16[1024,512]{1,0:T(8,128)(2,1)S(1)}, bf16[1024,512]{1,0:T(8,128)(2,1)}, u32[]{:S(2)}) copy-start(bf16[1024,512]{1,0:T(8,128)(2,1)} %param.24) | copy-start | bytes 3145732
  7.2 64.0 %reduce-scatter.9.cloned.1.call-start = ((), (), s32[]{:S(2)}) async-start(), calls=%async_computation.8 | async-start | bytes 4718592 | tf_op jit(solution)/shard_map/reduce_scatter | solution.py:39
  7.2 7.0 %collective-permute-start = (bf16[256,512]{1,0:T(8,128)(2,1)}, bf16[256,512]{1,0:T(8,128)(2,1)S(1)}, u32[]{:S(2)}, u32[]{:S(2)}) collective-permute-start(bf16[256,512]{1,0:T(8,128)(2,1)} %param.15), channel_id=1, source_target_pairs={{0,1},{1,2},{2,3},{3,0},{4,5},{5,6},{6,7},{7,4},{8,9},{9,10},{10,1... | collective-permute-start | bytes 786440 | tf_op jit(solution)/shard_map/ppermute | solution.py:24
  7.8 11.6 %collective-permute-start.1 = (bf16[256,512]{1,0:T(8,128)(2,1)}, bf16[256,512]{1,0:T(8,128)(2,1)S(1)}, u32[]{:S(2)}, u32[]{:S(2)}) collective-permute-start(bf16[256,512]{1,0:T(8,128)(2,1)} %param.15), channel_id=1, source_target_pairs={{0,3},{1,0},{2,1},{3,2},{4,7},{5,4},{6,5},{7,6},{8,11},{9,8},{10,9... | collective-permute-start | bytes 786440 | tf_op jit(solution)/shard_map/ppermute | solution.py:27
  14.2 5.9 collective-permute-start.2
  23.8 96.5 %reduce-scatter.11.cloned.1.call-start = ((), (), s32[]{:S(2)}) async-start(), calls=%async_computation.9 | async-start | bytes 2621440 | tf_op jit(solution)/shard_map/reduce_scatter | solution.py:52
  88.9 112.0 %reduce-scatter.13.cloned.1.call-start = ((), (), s32[]{:S(2)}) async-start(), calls=%async_computation.10 | async-start | bytes 6291456 | tf_op jit(solution)/shard_map/reduce_scatter | solution.py:39
  128.6 8.0 %collective-permute-start.3 = (bf16[256,512]{1,0:T(8,128)(2,1)S(1)}, bf16[256,512]{1,0:T(8,128)(2,1)S(1)}, u32[]{:S(2)}, u32[]{:S(2)}) collective-permute-start(bf16[256,512]{1,0:T(8,128)(2,1)S(1)} %get-tuple-element.71), channel_id=1, source_target_pairs={{0,1},{1,2},{2,3},{3,0},{4,5},{5,6},{6,7},{7,4},{8,9},{9,10},{10,1... | collective-permute-start | bytes 786440 | tf_op jit(solution)/shard_map/ppermute | solution.py:24
  128.6 8.0 %collective-permute-start.4 = (bf16[256,512]{1,0:T(8,128)(2,1)S(1)}, bf16[256,512]{1,0:T(8,128)(2,1)S(1)}, u32[]{:S(2)}, u32[]{:S(2)}) collective-permute-start(bf16[256,512]{1,0:T(8,128)(2,1)S(1)} %get-tuple-element.71), channel_id=1, source_target_pairs={{0,3},{1,0},{2,1},{3,2},{4,7},{5,4},{6,5},{7,6},{8,11},{9,8},{10,9... | collective-permute-start | bytes 786440 | tf_op jit(solution)/shard_map/ppermute | solution.py:27
  136.6 5.8 collective-permute-start.5
  146.6 54.3 %copy-start.27 = (f32[1024]{0:T(1024)S(1)}, f32[1024]{0:T(1024)}, u32[]{:S(2)}) copy-start(f32[1024]{0:T(1024)} %param.23) | copy-start | bytes 12292
  146.6 90.6 %all-gather.6.cloned.1.call-start = ((), (), s32[]{:S(2)}) async-start(), calls=%async_computation.11 | async-start | bytes 3145728 | tf_op jit(solution)/shard_map/all_gather | solution.py:48
  204.0 68.7 %reduce-scatter.15.cloned.1.call-start = ((), (), s32[]{:S(2)}) async-start(), calls=%async_computation.12 | async-start | bytes 2621440 | tf_op jit(solution)/shard_map/reduce_scatter | solution.py:52
  241.4 44.8 %copy-start.32 = (f32[512]{0:T(512)S(1)}, f32[512]{0:T(512)}, u32[]{:S(2)}) copy-start(f32[512]{0:T(512)} %param.27) | copy-start | bytes 6148
  241.4 65.3 %all-gather.8.cloned.1.call-start = ((), (), s32[]{:S(2)}) async-start(), calls=%async_computation.13 | async-start | bytes 1310720 | tf_op jit(solution)/shard_map/all_gather | solution.py:61
  289.9 75.9 %reduce-scatter.17.cloned.1.call-start = ((), (), s32[]{:S(2)}) async-start(), calls=%async_computation.14 | async-start | bytes 6291456 | tf_op jit(solution)/shard_map/reduce_scatter | solution.py:65
  311.2 91.3 %copy-start.36 = (bf16[512,1024]{1,0:T(8,128)(2,1)S(1)}, bf16[512,1024]{1,0:T(8,128)(2,1)}, u32[]{:S(2)}) copy-start(bf16[512,1024]{1,0:T(8,128)(2,1)} %param.22) | copy-start | bytes 3145732
  311.2 91.3 %all-gather.10.cloned.1.call-start = ((), (), s32[]{:S(2)}) async-start(), calls=%async_computation.15 | async-start | bytes 3145728 | tf_op jit(solution)/shard_map/all_gather | solution.py:74
  369.3 68.8 %reduce-scatter.19.cloned.1.call-start = ((), (), s32[]{:S(2)}) async-start(), calls=%async_computation.16 | async-start | bytes 2621440 | tf_op jit(solution)/shard_map/reduce_scatter | solution.py:78
  406.7 57.3 %all-gather.12.cloned.1.call-start = ((), (), s32[]{:S(2)}) async-start(), calls=%async_computation.17 | async-start | bytes 1310720 | tf_op jit(solution)/shard_map/all_gather | solution.py:61
  447.1 40.1 %reduce-scatter.21.cloned.1.call-start = ((), (), s32[]{:S(2)}) async-start(), calls=%async_computation.18 | async-start | bytes 1572864 | tf_op jit(solution)/shard_map/reduce_scatter | solution.py:65
  466.8 57.9 %all-gather.14.cloned.1.call-start = ((), (), s32[]{:S(2)}) async-start(), calls=%async_computation.19 | async-start | bytes 2359296 | tf_op jit(solution)/shard_map/all_gather | solution.py:74
  497.3 153.2 %all-reduce.9.cloned.1.call-start = ((), (), s32[]{:S(2)}) async-start(), calls=%async_computation.21 | async-start | bytes 6291456 | tf_op jit(solution)/shard_map/psum | solution.py:297
  528.3 154.9 %reduce-scatter.23.cloned.1.call-start = ((), (), s32[]{:S(2)}) async-start(), calls=%async_computation.20 | async-start | bytes 2621440 | tf_op jit(solution)/shard_map/reduce_scatter | solution.py:78
  (34 other events, 436.3 us)
Sparse Core Ops, SparseCore 0:
  23.9 47.2 reduce-scatter.8
  89.1 31.1 reduce-scatter.10
  146.8 54.1 reduce-scatter.12
  204.1 33.0 all-gather.5
  241.6 31.1 reduce-scatter.14
  290.0 16.6 all-gather.7
  311.4 54.3 reduce-scatter.16
  369.4 33.0 all-gather.9
  406.9 31.1 reduce-scatter.18
  447.3 16.7 all-gather.11
  466.9 20.3 reduce-scatter.20
  497.4 27.1 all-gather.13
  528.4 122.0 all-reduce.8
  652.9 30.2 reduce-scatter.22
